TPU v7x, 32 devices: a whole 2x2x4 slice. The times are simulated.
32 devices in a mesh: tx: 8 (over z, x), ty: 4 (over y, core).
Axes of the slice: x: 2, y: 2, z: 4, core: 2. Of those that a mesh axis runs over, the one named last changes fastest.
Arguments:
- dynamics_residual: float32 [6, 48, 48, 16], P(None, 'tx', 'ty'), may hold values from -6 to 6
- density: float32 [6, 48, 48, 16], P(None, 'tx', 'ty'), may hold values from 0.5 to 8
- diagonal_gain: float32 [6, 48, 48, 16], P(None, 'tx', 'ty'), may hold values from 0.05 to 2
- vertical_coupling: float32 [6, 48, 48, 16], P(None, 'tx', 'ty'), may hold values from 0.2 to 8
- edge_panel: int32 [6, 4], replicated, may hold values from 0 to 5, as said below
- edge_side: int32 [6, 4], replicated, may hold values from 0 to 3, as said below
- edge_flip: int32 [6, 4], replicated, may hold values from 0 to 1, as said below
Outputs:
- solution: float32 [6, 48, 48, 16], P(None, 'tx', 'ty')
- coarse_correction: float32 [6, 24, 24, 16], P(None, 'tx', 'ty')
Inputs may be any that keep to these rules, and one draw needn't show every extreme that they name: The six panels are the faces of a cube, each with its own orientation and label: side s of panel p borders side edge_side[p, s] of panel edge_panel[p, s], the pairing is mutual, and no side borders a side of its own panel. `edge_side`: see edge_panel. `edge_flip`: equal on both sides of a bordering pair.
All inputs are finite; a program needn't handle non-finite values.
Results may differ from a plain program's by a relative error of at most 0.00005.
Values sent between devices are 32-bit elements; how exact they have to be, the bound alone decides.
A program may use at most 64 MiB of HBM per device.

v0:
```python
import jax
import jax.numpy as jnp
from jax import lax
from jax.sharding import PartitionSpec as P

relaxation = 0.8
highest = lax.Precision.HIGHEST


def extended(x, sides, width):
    for axis, dim in sides:
        count, length = (lax.axis_size(axis), x.shape[dim])
        up = [(i, (i + 1) % count) for i in range(count - 1)]
        down = [(j, i) for i, j in up]
        last = lax.slice_in_dim(x, length - width, length, axis=dim)
        first = lax.slice_in_dim(x, 0, width, axis=dim)
        before = lax.ppermute(last, axis, up)
        after = lax.ppermute(first, axis, down)
        x = jnp.concatenate([before, x, after], axis=dim)
    return x


def partner(value, axis, distance):
    mask = 2**distance
    pairs = [(source, source ^ mask) for source in range(lax.axis_size(axis))]
    return lax.ppermute(value, axis, pairs)


def lower_levels(values):
    return jnp.concatenate([jnp.zeros_like(values[..., :1]), values[..., :-1]], axis=-1)


def upper_levels(values):
    return jnp.concatenate([values[..., 1:], jnp.zeros_like(values[..., :1])], axis=-1)


def vertical_part(grid_field, vertical):
    return vertical * (grid_field - upper_levels(grid_field)) + lower_levels(vertical) * (
        grid_field - lower_levels(grid_field)
    )


def diagonal_of(cell_gain, vertical, horizontal):
    return cell_gain + 4.0 * horizontal + vertical + lower_levels(vertical)


def neighbour_sum(padded):
    return padded[:, :-2, 1:-1] + padded[:, 2:, 1:-1] + padded[:, 1:-1, :-2] + padded[:, 1:-1, 2:]


def apply_operator(grid_field, padded, cell_gain, vertical, horizontal):
    return (
        cell_gain * grid_field
        + horizontal * (4.0 * grid_field - neighbour_sum(padded))
        + vertical_part(grid_field, vertical)
    )


def restrict(values):
    shaped = values.reshape(
        values.shape[0], values.shape[1] // 2, 2, values.shape[2] // 2, 2, values.shape[3]
    )
    return shaped.mean(axis=(2, 4))


def prolong(values):
    return jnp.repeat(jnp.repeat(values, 2, axis=1), 2, axis=2)


def window_piece(held_block, positions, offset):
    length = held_block.shape[2]
    local_index = positions - offset
    inside = ((local_index >= 0) & (local_index < length)).astype(jnp.float32)
    picked = jnp.take(held_block, jnp.clip(local_index, 0, length - 1), axis=2)
    return picked * inside[None, None, :, None]


def select_rims(forward, mirrored, edge_panel, edge_side, edge_flip, first_side):
    side_codes = edge_side[:, first_side : first_side + 2]
    panel_codes = edge_panel[:, first_side : first_side + 2]
    flip_codes = edge_flip[:, first_side : first_side + 2].astype(jnp.float32)
    matched = (
        (side_codes[:, :, None, None] == jnp.arange(4)[None, None, :, None])
        & (panel_codes[:, :, None, None] == jnp.arange(6)[None, None, None, :])
    ).astype(jnp.float32)
    straight = matched * (1.0 - flip_codes)[:, :, None, None]
    turned = matched * flip_codes[:, :, None, None]
    return jnp.einsum("pstq,tqjl->psjl", straight, forward, precision=highest) + jnp.einsum(
        "pstq,tqjl->psjl", turned, mirrored, precision=highest
    )


def padded_tile(grid_field, edge_panel, edge_side, edge_flip):
    row_index = lax.axis_index("tx")
    col_index = lax.axis_index("ty")
    row_count = lax.axis_size("tx")
    col_count = lax.axis_size("ty")
    tile_rows = grid_field.shape[1]
    tile_cols = grid_field.shape[2]
    side_cells = tile_rows * row_count
    padded = extended(grid_field, (("tx", 1), ("ty", 2)), 1)
    across_mask = jnp.stack([row_index == 0, row_index == row_count - 1]).astype(jnp.float32)
    along_mask = jnp.stack([col_index == 0, col_index == col_count - 1]).astype(jnp.float32)
    row_sides = jnp.stack([grid_field[:, 0], grid_field[:, -1]]) * across_mask[:, None, None, None]
    col_sides = (
        jnp.stack([grid_field[:, :, 0], grid_field[:, :, -1]]) * along_mask[:, None, None, None]
    )
    col_block = lax.psum(row_sides, "tx")
    row_block = lax.psum(col_sides, "ty")
    col_positions = col_index * tile_cols + jnp.arange(tile_cols)
    row_positions = row_index * tile_rows + jnp.arange(tile_rows)
    cross_cols = jnp.stack(
        [
            window_piece(row_block, col_positions, row_index * tile_rows),
            window_piece(row_block, side_cells - 1 - col_positions, row_index * tile_rows),
        ]
    )
    summed_cols = lax.psum(cross_cols, "tx")
    cross_rows = jnp.stack(
        [
            window_piece(col_block, row_positions, col_index * tile_cols),
            window_piece(col_block, side_cells - 1 - row_positions, col_index * tile_cols),
        ]
    )
    summed_rows = lax.psum(cross_rows, "ty")
    mirror_rowblock = row_block[:, :, ::-1]
    for bit in range(row_count.bit_length() - 1):
        mirror_rowblock = partner(mirror_rowblock, "tx", bit)
    mirror_colblock = col_block[:, :, ::-1]
    for bit in range(col_count.bit_length() - 1):
        mirror_colblock = partner(mirror_colblock, "ty", bit)
    cols_forward = jnp.concatenate([col_block, summed_cols[0]], axis=0)
    cols_mirror = jnp.concatenate([mirror_colblock, summed_cols[1]], axis=0)
    rows_forward = jnp.concatenate([summed_rows[0], row_block], axis=0)
    rows_mirror = jnp.concatenate([summed_rows[1], mirror_rowblock], axis=0)
    col_rims = select_rims(cols_forward, cols_mirror, edge_panel, edge_side, edge_flip, 0)
    row_rims = select_rims(rows_forward, rows_mirror, edge_panel, edge_side, edge_flip, 2)
    top_rim = jnp.where(row_index == 0, col_rims[:, 0], padded[:, 0, 1:-1])
    bottom_rim = jnp.where(row_index == row_count - 1, col_rims[:, 1], padded[:, -1, 1:-1])
    left_rim = jnp.where(col_index == 0, row_rims[:, 0], padded[:, 1:-1, 0])
    right_rim = jnp.where(col_index == col_count - 1, row_rims[:, 1], padded[:, 1:-1, -1])
    padded = padded.at[:, 0, 1:-1].set(top_rim)
    padded = padded.at[:, -1, 1:-1].set(bottom_rim)
    padded = padded.at[:, 1:-1, 0].set(left_rim)
    padded = padded.at[:, 1:-1, -1].set(right_rim)
    return padded


def shards(
    dynamics_residual, density, diagonal_gain, vertical_coupling, edge_panel, edge_side, edge_flip
):
    right_side = density * dynamics_residual
    fine_diagonal = diagonal_of(diagonal_gain, vertical_coupling, 1.0)
    smoothed = relaxation * right_side / fine_diagonal
    applied = apply_operator(
        smoothed,
        padded_tile(smoothed, edge_panel, edge_side, edge_flip),
        diagonal_gain,
        vertical_coupling,
        1.0,
    )
    coarse_rhs = restrict(right_side - applied)
    coarse_gain = restrict(diagonal_gain)
    coarse_vertical = restrict(vertical_coupling)
    coarse_diagonal = diagonal_of(coarse_gain, coarse_vertical, 0.25)
    coarse_guess = relaxation * coarse_rhs / coarse_diagonal
    coarse_applied = apply_operator(
        coarse_guess,
        padded_tile(coarse_guess, edge_panel, edge_side, edge_flip),
        coarse_gain,
        coarse_vertical,
        0.25,
    )
    coarse_correction = coarse_guess + relaxation * (coarse_rhs - coarse_applied) / coarse_diagonal
    corrected = smoothed + prolong(coarse_correction)
    final_applied = apply_operator(
        corrected,
        padded_tile(corrected, edge_panel, edge_side, edge_flip),
        diagonal_gain,
        vertical_coupling,
        1.0,
    )
    solution = corrected + relaxation * (right_side - final_applied) / fine_diagonal
    return (solution, coarse_correction)


def solution(mesh):
    placed = (
        P(None, "tx", "ty", None),
        P(None, "tx", "ty", None),
        P(None, "tx", "ty", None),
        P(None, "tx", "ty", None),
        P(),
        P(),
        P(),
    )
    return jax.shard_map(
        shards,
        mesh=mesh,
        in_specs=placed,
        out_specs=(P(None, "tx", "ty", None), P(None, "tx", "ty", None)),
        check_vma=False,
    )
```

profile of v0, /device:TPU:0, one launch (start us, length us, event | category | flops | bytes accessed | tf_op | source)
XLA Modules:
  0.0 281.6 jit_solution(7349908816677631455)
XLA Ops:
  3.6 13.3 %psum.85 = f32[2,6,6,16]{3,1,0,2:T(8,128)S(1)} all-reduce(f32[2,6,6,16]{3,1,0,2:T(8,128)S(1)} %maximum_multiply_fusion.2), channel_id=1, replica_groups=mesh['tx'=8,'ty'=4] {'ty'}, use_global_device_ids=true, to_apply=%region_1.0 | all-reduce | flops 1152 | bytes 9216 | tf_op jit(solution)/shard_map/psum | solution.py:109
  19.8 4.5 %collective-permute-start = (f32[6,1,12,16]{3,0,2,1:T(8,128)S(1)}, f32[6,1,12,16]{3,0,2,1:T(8,128)S(1)}, u32[]{:S(2)}, u32[]{:S(2)}) collective-permute-start(f32[6,1,12,16]{3,0,2,1:T(8,128)S(1)} %get-tuple-element.193), channel_id=1, source_target_pairs={{0,4},{4,8},{8,12},{12,16},{16,20},{20,24},{24,28},{1,5},{5,9},{9,... | collective-permute-start | bytes 13832 | tf_op jit(solution)/shard_map/ppermute | solution.py:17
  25.9 38.7 %all-reduce.10 = (f32[2,2,6,12,16]{4,2,1,3,0:T(8,128)S(1)}, f32[2,6,12,16]{3,1,0,2:T(8,128)S(1)}) all-reduce(f32[2,2,6,12,16]{4,2,1,3,0:T(8,128)S(1)} %pad_maximum_fusion.2, f32[2,6,12,16]{3,1,0,2:T(8,128)S(1)} %copy.51), channel_id=1, replica_groups=mesh['tx'=8,'ty'=4] {'tx'}, use_global_device_ids=true, to_apply=%region_2.4 | all-reduce | flops 6912 | bytes 55296 | tf_op jit(solution)/shard_map/psum | solution.py:118
  69.0 11.5 %psum.87 = f32[2,2,6,6,16]{4,2,1,3,0:T(8,128)S(1)} all-reduce(f32[2,2,6,6,16]{4,2,1,3,0:T(8,128)S(1)} %pad_maximum_fusion.5), channel_id=1, replica_groups=mesh['tx'=8,'ty'=4] {'ty'}, use_global_device_ids=true, to_apply=%region_3.6 | all-reduce | flops 2304 | bytes 18432 | tf_op jit(solution)/shard_map/psum | solution.py:125
  81.6 2.0 collective-permute-start.2
  85.3 3.7 %collective-permute-done.7 = f32[2,6,6,16]{3,1,0,2:T(8,128)S(1)} collective-permute-done((f32[2,6,6,16]{3,1,0,2:T(8,128)S(1)}, f32[2,6,6,16]{3,1,0,2:T(8,128)S(1)}, u32[]{:S(2)}, u32[]{:S(2)}) %collective-permute-start.7) | collective-permute-done | bytes 4640 | tf_op jit(solution)/shard_map/ppermute | solution.py:26
  89.2 4.0 %collective-permute-start.5 = (f32[2,6,12,16]{3,1,0,2:T(8,128)S(1)}, f32[2,6,12,16]{3,1,0,2:T(8,128)S(1)}, u32[]{:S(2)}, u32[]{:S(2)}) collective-permute-start(f32[2,6,12,16]{3,1,0,2:T(8,128)S(1)} %collective-permute-done.4), channel_id=1, source_target_pairs={{0,2},{1,3},{2,0},{3,1},{4,6},{5,7},{6,4},{7,5},{8,10},{9,11},{10,... | collective-permute-start | bytes 27656 | tf_op jit(solution)/shard_map/ppermute | solution.py:26
  93.1 2.0 collective-permute-done.8
  98.8 10.7 %psum.89 = f32[2,6,3,16]{3,1,0,2:T(8,128)S(1)} all-reduce(f32[2,6,3,16]{3,1,0,2:T(8,128)S(1)} %maximum_multiply_fusion.4), channel_id=1, replica_groups=mesh['tx'=8,'ty'=4] {'ty'}, use_global_device_ids=true, to_apply=%region_8.11 | all-reduce | flops 576 | bytes 4608 | tf_op jit(solution)/shard_map/psum | solution.py:109
  111.0 37.9 %all-reduce.9 = (f32[2,2,6,6,16]{4,2,1,3,0:T(8,128)S(1)}, f32[2,6,6,16]{3,1,0,2:T(8,128)S(1)}) all-reduce(f32[2,2,6,6,16]{4,2,1,3,0:T(8,128)S(1)} %pad_maximum_fusion.6, f32[2,6,6,16]{3,1,0,2:T(8,128)S(1)} %copy.60), channel_id=1, replica_groups=mesh['tx'=8,'ty'=4] {'tx'}, use_global_device_ids=true, to_apply=%region_9.13 | all-reduce | flops 3456 | bytes 27648 | tf_op jit(solution)/shard_map/psum | solution.py:118
  150.3 10.5 %psum.91 = f32[2,2,6,3,16]{4,2,1,3,0:T(8,128)S(1)} all-reduce(f32[2,2,6,3,16]{4,2,1,3,0:T(8,128)S(1)} %pad_maximum_fusion.8), channel_id=1, replica_groups=mesh['tx'=8,'ty'=4] {'ty'}, use_global_device_ids=true, to_apply=%region_10.15 | all-reduce | flops 1152 | bytes 9216 | tf_op jit(solution)/shard_map/psum | solution.py:125
  162.1 4.5 %collective-permute-start.9 = (f32[6,1,6,16]{3,0,2,1:T(8,128)S(1)}, f32[6,1,6,16]{3,0,2,1:T(8,128)S(1)}, u32[]{:S(2)}, u32[]{:S(2)}) collective-permute-start(f32[6,1,6,16]{3,0,2,1:T(8,128)S(1)} %get-tuple-element.213), channel_id=1, source_target_pairs={{0,4},{4,8},{8,12},{12,16},{16,20},{20,24},{24,28},{1,5},{5,9},{9,... | collective-permute-start | bytes 6920 | tf_op jit(solution)/shard_map/ppermute | solution.py:17
  170.8 1.8 collective-permute-start.16
  173.0 3.2 %collective-permute-start.13 = (f32[2,6,6,16]{3,1,0,2:T(8,128)S(1)}, f32[2,6,6,16]{3,1,0,2:T(8,128)S(1)}, u32[]{:S(2)}, u32[]{:S(2)}) collective-permute-start(f32[2,6,6,16]{3,1,0,2:T(8,128)S(1)} %rev.20), channel_id=1, source_target_pairs={{0,1},{1,0},{2,3},{3,2},{4,5},{5,4},{6,7},{7,6},{8,9},{9,8},{10,11... | collective-permute-start | bytes 13832 | tf_op jit(solution)/shard_map/ppermute | solution.py:26
  177.1 2.9 %collective-permute-start.14 = (f32[2,6,6,16]{3,1,0,2:T(8,128)S(1)}, f32[2,6,6,16]{3,1,0,2:T(8,128)S(1)}, u32[]{:S(2)}, u32[]{:S(2)}) collective-permute-start(f32[2,6,6,16]{3,1,0,2:T(8,128)S(1)} %collective-permute-done.13), channel_id=1, source_target_pairs={{0,2},{1,3},{2,0},{3,1},{4,6},{5,7},{6,4},{7,5},{8,10},{9,11},{10,... | collective-permute-start | bytes 13832 | tf_op jit(solution)/shard_map/ppermute | solution.py:26
  184.2 11.0 %psum.93 = f32[2,6,6,16]{3,1,0,2:T(8,128)S(1)} all-reduce(f32[2,6,6,16]{3,1,0,2:T(8,128)S(1)} %copy_multiply_fusion.3), channel_id=1, replica_groups=mesh['tx'=8,'ty'=4] {'ty'}, use_global_device_ids=true, to_apply=%region_12.17 | all-reduce | flops 1152 | bytes 9216 | tf_op jit(solution)/shard_map/psum | solution.py:109
  197.9 39.3 %all-reduce.8 = (f32[2,2,6,12,16]{4,2,1,3,0:T(8,128)S(1)}, f32[2,6,12,16]{3,1,0,2:T(8,128)S(1)}) all-reduce(f32[2,2,6,12,16]{4,2,1,3,0:T(8,128)S(1)} %pad_maximum_fusion.3, f32[2,6,12,16]{3,1,0,2:T(8,128)S(1)} %copy.67), channel_id=1, replica_groups=mesh['tx'=8,'ty'=4] {'tx'}, use_global_device_ids=true, to_apply=%region_13.18 | all-reduce | flops 6912 | bytes 55296 | tf_op jit(solution)/shard_map/psum | solution.py:118
  238.8 11.1 %psum.95 = f32[2,2,6,6,16]{4,2,1,3,0:T(8,128)S(1)} all-reduce(f32[2,2,6,6,16]{4,2,1,3,0:T(8,128)S(1)} %pad_maximum_fusion.7), channel_id=1, replica_groups=mesh['tx'=8,'ty'=4] {'ty'}, use_global_device_ids=true, to_apply=%region_14.19 | all-reduce | flops 2304 | bytes 18432 | tf_op jit(solution)/shard_map/psum | solution.py:125
  252.0 4.7 %collective-permute-start.18 = (f32[6,1,12,16]{3,0,2,1:T(8,128)S(1)}, f32[6,1,12,16]{3,0,2,1:T(8,128)S(1)}, u32[]{:S(2)}, u32[]{:S(2)}) collective-permute-start(f32[6,1,12,16]{3,0,2,1:T(8,128)S(1)} %copy-done.4), channel_id=1, source_target_pairs={{0,4},{4,8},{8,12},{12,16},{16,20},{20,24},{24,28},{1,5},{5,9},{9,... | collective-permute-start | bytes 13832 | tf_op jit(solution)/shard_map/ppermute | solution.py:17
  258.5 1.6 collective-permute-start.20
  261.4 4.4 %collective-permute-start.25 = (f32[2,6,6,16]{3,1,0,2:T(8,128)}, f32[2,6,6,16]{3,1,0,2:T(8,128)}, u32[]{:S(2)}, u32[]{:S(2)}) collective-permute-start(f32[2,6,6,16]{3,1,0,2:T(8,128)} %collective-permute-done.24), channel_id=1, source_target_pairs={{0,8},{4,12},{8,0},{12,4},{16,24},{20,28},{24,16},{28,20},{1,9},{5... | collective-permute-start | bytes 13832 | tf_op jit(solution)/shard_map/ppermute | solution.py:26
  267.6 3.3 %collective-permute-start.22 = (f32[2,6,12,16]{3,1,0,2:T(8,128)}, f32[2,6,12,16]{3,1,0,2:T(8,128)S(1)}, u32[]{:S(2)}, u32[]{:S(2)}) collective-permute-start(f32[2,6,12,16]{3,1,0,2:T(8,128)} %rev.22), channel_id=1, source_target_pairs={{0,1},{1,0},{2,3},{3,2},{4,5},{5,4},{6,7},{7,6},{8,9},{9,8},{10,11... | collective-permute-start | bytes 27656 | tf_op jit(solution)/shard_map/ppermute | solution.py:26
  272.0 2.3 collective-permute-start.23
  274.3 2.6 collective-permute-done.26
  (215 shorter events, 48.0 us)
Async XLA Ops:
  16.9 68.0 %collective-permute-start.6 = (f32[2,6,6,16]{3,1,0,2:T(8,128)S(1)}, f32[2,6,6,16]{3,1,0,2:T(8,128)S(1)}, u32[]{:S(2)}, u32[]{:S(2)}) collective-permute-start(f32[2,6,6,16]{3,1,0,2:T(8,128)S(1)} %rev.19), channel_id=1, source_target_pairs={{0,4},{4,0},{8,12},{12,8},{16,20},{20,16},{24,28},{28,24},{1,5},{5... | collective-permute-start | bytes 13832 | tf_op jit(solution)/shard_map/ppermute | solution.py:26
  18.5 63.1 %collective-permute-start.1 = (f32[6,1,12,16]{3,0,2,1:T(8,128)S(1)}, f32[6,1,12,16]{3,0,2,1:T(8,128)S(1)}, u32[]{:S(2)}, u32[]{:S(2)}) collective-permute-start(f32[6,1,12,16]{3,0,2,1:T(8,128)S(1)} %get-tuple-element.192), channel_id=1, source_target_pairs={{4,0},{8,4},{12,8},{16,12},{20,16},{24,20},{28,24},{5,1},{9,5},{13... | collective-permute-start | bytes 13832 | tf_op jit(solution)/shard_map/ppermute | solution.py:18
  19.8 61.8 %collective-permute-start = (f32[6,1,12,16]{3,0,2,1:T(8,128)S(1)}, f32[6,1,12,16]{3,0,2,1:T(8,128)S(1)}, u32[]{:S(2)}, u32[]{:S(2)}) collective-permute-start(f32[6,1,12,16]{3,0,2,1:T(8,128)S(1)} %get-tuple-element.193), channel_id=1, source_target_pairs={{0,4},{4,8},{8,12},{12,16},{16,20},{20,24},{24,28},{1,5},{5,9},{9,... | collective-permute-start | bytes 13832 | tf_op jit(solution)/shard_map/ppermute | solution.py:17
  64.7 24.5 %collective-permute-start.4 = (f32[2,6,12,16]{3,1,0,2:T(8,128)S(1)}, f32[2,6,12,16]{3,1,0,2:T(8,128)S(1)}, u32[]{:S(2)}, u32[]{:S(2)}) collective-permute-start(f32[2,6,12,16]{3,1,0,2:T(8,128)S(1)} %rev.18), channel_id=1, source_target_pairs={{0,1},{1,0},{2,3},{3,2},{4,5},{5,4},{6,7},{7,6},{8,9},{9,8},{10,11... | collective-permute-start | bytes 27656 | tf_op jit(solution)/shard_map/ppermute | solution.py:26
  81.6 7.5 %collective-permute-start.2 = (f32[6,8,1,16]{3,0,1,2:T(8,128)S(1)}, f32[6,8,1,16]{3,0,1,2:T(8,128)S(1)}, u32[]{:S(2)}, u32[]{:S(2)}) collective-permute-start(f32[6,8,1,16]{3,0,1,2:T(8,128)S(1)} %get-tuple-element.178), channel_id=1, source_target_pairs={{0,1},{1,2},{2,3},{4,5},{5,6},{6,7},{8,9},{9,10},{10,11},{12,13},{... | collective-permute-start | bytes 9224 | tf_op jit(solution)/shard_map/ppermute | solution.py:17
  83.6 5.5 %collective-permute-start.3 = (f32[6,8,1,16]{3,0,1,2:T(8,128)S(1)}, f32[6,8,1,16]{3,0,1,2:T(8,128)S(1)}, u32[]{:S(2)}, u32[]{:S(2)}) collective-permute-start(f32[6,8,1,16]{3,0,1,2:T(8,128)S(1)} %get-tuple-element.179), channel_id=1, source_target_pairs={{1,0},{2,1},{3,2},{5,4},{6,5},{7,6},{9,8},{10,9},{11,10},{13,12},{... | collective-permute-start | bytes 9224 | tf_op jit(solution)/shard_map/ppermute | solution.py:18
  89.1 6.0 %collective-permute-start.8 = (f32[2,6,6,16]{3,1,0,2:T(8,128)S(1)}, f32[2,6,6,16]{3,1,0,2:T(8,128)S(1)}, u32[]{:S(2)}, u32[]{:S(2)}) collective-permute-start(f32[2,6,6,16]{3,1,0,2:T(8,128)S(1)} %collective-permute-done.7), channel_id=1, source_target_pairs={{0,16},{4,20},{8,24},{12,28},{16,0},{20,4},{24,8},{28,12},{1,17},{... | collective-permute-start | bytes 13832 | tf_op jit(solution)/shard_map/ppermute | solution.py:26
  89.2 6.6 %collective-permute-start.5 = (f32[2,6,12,16]{3,1,0,2:T(8,128)S(1)}, f32[2,6,12,16]{3,1,0,2:T(8,128)S(1)}, u32[]{:S(2)}, u32[]{:S(2)}) collective-permute-start(f32[2,6,12,16]{3,1,0,2:T(8,128)S(1)} %collective-permute-done.4), channel_id=1, source_target_pairs={{0,2},{1,3},{2,0},{3,1},{4,6},{5,7},{6,4},{7,5},{8,10},{9,11},{10,... | collective-permute-start | bytes 27656 | tf_op jit(solution)/shard_map/ppermute | solution.py:26
  109.5 61.2 %collective-permute-start.15 = (f32[2,6,3,16]{3,1,0,2:T(8,128)S(1)}, f32[2,6,3,16]{3,1,0,2:T(8,128)S(1)}, u32[]{:S(2)}, u32[]{:S(2)}) collective-permute-start(f32[2,6,3,16]{3,1,0,2:T(8,128)S(1)} %rev.21), channel_id=1, source_target_pairs={{0,4},{4,0},{8,12},{12,8},{16,20},{20,16},{24,28},{28,24},{1,5},{5... | collective-permute-start | bytes 6920 | tf_op jit(solution)/shard_map/ppermute | solution.py:26
  160.8 6.3 %collective-permute-start.10 = (f32[6,1,6,16]{3,0,1,2:T(8,128)S(1)}, f32[6,1,6,16]{3,0,1,2:T(8,128)S(1)}, u32[]{:S(2)}, u32[]{:S(2)}) collective-permute-start(f32[6,1,6,16]{3,0,1,2:T(8,128)S(1)} %get-tuple-element.212), channel_id=1, source_target_pairs={{4,0},{8,4},{12,8},{16,12},{20,16},{24,20},{28,24},{5,1},{9,5},{13... | collective-permute-start | bytes 6920 | tf_op jit(solution)/shard_map/ppermute | solution.py:18
  162.1 6.1 %collective-permute-start.9 = (f32[6,1,6,16]{3,0,2,1:T(8,128)S(1)}, f32[6,1,6,16]{3,0,2,1:T(8,128)S(1)}, u32[]{:S(2)}, u32[]{:S(2)}) collective-permute-start(f32[6,1,6,16]{3,0,2,1:T(8,128)S(1)} %get-tuple-element.213), channel_id=1, source_target_pairs={{0,4},{4,8},{8,12},{12,16},{16,20},{20,24},{24,28},{1,5},{5,9},{9,... | collective-permute-start | bytes 6920 | tf_op jit(solution)/shard_map/ppermute | solution.py:17
  168.2 8.6 %collective-permute-start.11 = (f32[6,5,1,16]{3,0,1,2:T(8,128)S(1)}, f32[6,5,1,16]{3,0,1,2:T(8,128)S(1)}, u32[]{:S(2)}, u32[]{:S(2)}) collective-permute-start(f32[6,5,1,16]{3,0,1,2:T(8,128)S(1)} %get-tuple-element.200), channel_id=1, source_target_pairs={{0,1},{1,2},{2,3},{4,5},{5,6},{6,7},{8,9},{9,10},{10,11},{12,13},{... | collective-permute-start | bytes 5768 | tf_op jit(solution)/shard_map/ppermute | solution.py:17
  169.4 7.3 %collective-permute-start.12 = (f32[6,5,1,16]{3,0,1,2:T(8,128)S(1)}, f32[6,5,1,16]{3,0,1,2:T(8,128)S(1)}, u32[]{:S(2)}, u32[]{:S(2)}) collective-permute-start(f32[6,5,1,16]{3,0,1,2:T(8,128)S(1)} %get-tuple-element.201), channel_id=1, source_target_pairs={{1,0},{2,1},{3,2},{5,4},{6,5},{7,6},{9,8},{10,9},{11,10},{13,12},{... | collective-permute-start | bytes 5768 | tf_op jit(solution)/shard_map/ppermute | solution.py:18
  170.8 5.5 %collective-permute-start.16 = (f32[2,6,3,16]{3,1,0,2:T(8,128)S(1)}, f32[2,6,3,16]{3,1,0,2:T(8,128)S(1)}, u32[]{:S(2)}, u32[]{:S(2)}) collective-permute-start(f32[2,6,3,16]{3,1,0,2:T(8,128)S(1)} %collective-permute-done.15), channel_id=1, source_target_pairs={{0,8},{4,12},{8,0},{12,4},{16,24},{20,28},{24,16},{28,20},{1,9},{5... | collective-permute-start | bytes 6920 | tf_op jit(solution)/shard_map/ppermute | solution.py:26
  176.3 5.0 %collective-permute-start.17 = (f32[2,6,3,16]{3,1,0,2:T(8,128)S(1)}, f32[2,6,3,16]{3,1,0,2:T(8,128)S(1)}, u32[]{:S(2)}, u32[]{:S(2)}) collective-permute-start(f32[2,6,3,16]{3,1,0,2:T(8,128)S(1)} %collective-permute-done.16), channel_id=1, source_target_pairs={{0,16},{4,20},{8,24},{12,28},{16,0},{20,4},{24,8},{28,12},{1,17},{... | collective-permute-start | bytes 6920 | tf_op jit(solution)/shard_map/ppermute | solution.py:26
  177.1 5.0 %collective-permute-start.14 = (f32[2,6,6,16]{3,1,0,2:T(8,128)S(1)}, f32[2,6,6,16]{3,1,0,2:T(8,128)S(1)}, u32[]{:S(2)}, u32[]{:S(2)}) collective-permute-start(f32[2,6,6,16]{3,1,0,2:T(8,128)S(1)} %collective-permute-done.13), channel_id=1, source_target_pairs={{0,2},{1,3},{2,0},{3,1},{4,6},{5,7},{6,4},{7,5},{8,10},{9,11},{10,... | collective-permute-start | bytes 13832 | tf_op jit(solution)/shard_map/ppermute | solution.py:26
  238.5 22.9 %collective-permute-start.24 = (f32[2,6,6,16]{3,1,0,2:T(8,128)}, f32[2,6,6,16]{3,1,0,2:T(8,128)}, u32[]{:S(2)}, u32[]{:S(2)}) collective-permute-start(f32[2,6,6,16]{3,1,0,2:T(8,128)} %rev.23), channel_id=1, source_target_pairs={{0,4},{4,0},{8,12},{12,8},{16,20},{20,16},{24,28},{28,24},{1,5},{5... | collective-permute-start | bytes 13832 | tf_op jit(solution)/shard_map/ppermute | solution.py:26
  250.7 6.7 %collective-permute-start.19 = (f32[6,1,12,16]{3,0,1,2:T(8,128)S(1)}, f32[6,1,12,16]{3,0,1,2:T(8,128)S(1)}, u32[]{:S(2)}, u32[]{:S(2)}) collective-permute-start(f32[6,1,12,16]{3,0,1,2:T(8,128)S(1)} %copy-done.5), channel_id=1, source_target_pairs={{4,0},{8,4},{12,8},{16,12},{20,16},{24,20},{28,24},{5,1},{9,5},{13... | collective-permute-start | bytes 13832 | tf_op jit(solution)/shard_map/ppermute | solution.py:18
  252.0 6.5 %collective-permute-start.18 = (f32[6,1,12,16]{3,0,2,1:T(8,128)S(1)}, f32[6,1,12,16]{3,0,2,1:T(8,128)S(1)}, u32[]{:S(2)}, u32[]{:S(2)}) collective-permute-start(f32[6,1,12,16]{3,0,2,1:T(8,128)S(1)} %copy-done.4), channel_id=1, source_target_pairs={{0,4},{4,8},{8,12},{12,16},{16,20},{20,24},{24,28},{1,5},{5,9},{9,... | collective-permute-start | bytes 13832 | tf_op jit(solution)/shard_map/ppermute | solution.py:17
  258.5 12.4 %collective-permute-start.20 = (f32[6,8,1,16]{3,0,1,2:T(8,128)S(1)}, f32[6,8,1,16]{3,0,1,2:T(8,128)S(1)}, u32[]{:S(2)}, u32[]{:S(2)}) collective-permute-start(f32[6,8,1,16]{3,0,1,2:T(8,128)S(1)} %get-tuple-element.176), channel_id=1, source_target_pairs={{0,1},{1,2},{2,3},{4,5},{5,6},{6,7},{8,9},{9,10},{10,11},{12,13},{... | collective-permute-start | bytes 9224 | tf_op jit(solution)/shard_map/ppermute | solution.py:17
  260.1 10.8 %collective-permute-start.21 = (f32[6,8,1,16]{3,0,1,2:T(8,128)S(1)}, f32[6,8,1,16]{3,0,1,2:T(8,128)S(1)}, u32[]{:S(2)}, u32[]{:S(2)}) collective-permute-start(f32[6,8,1,16]{3,0,1,2:T(8,128)S(1)} %get-tuple-element.177), channel_id=1, source_target_pairs={{1,0},{2,1},{3,2},{5,4},{6,5},{7,6},{9,8},{10,9},{11,10},{13,12},{... | collective-permute-start | bytes 9224 | tf_op jit(solution)/shard_map/ppermute | solution.py:18
  261.4 9.5 %collective-permute-start.25 = (f32[2,6,6,16]{3,1,0,2:T(8,128)}, f32[2,6,6,16]{3,1,0,2:T(8,128)}, u32[]{:S(2)}, u32[]{:S(2)}) collective-permute-start(f32[2,6,6,16]{3,1,0,2:T(8,128)} %collective-permute-done.24), channel_id=1, source_target_pairs={{0,8},{4,12},{8,0},{12,4},{16,24},{20,28},{24,16},{28,20},{1,9},{5... | collective-permute-start | bytes 13832 | tf_op jit(solution)/shard_map/ppermute | solution.py:26
  270.9 6.0 %collective-permute-start.26 = (f32[2,6,6,16]{3,1,0,2:T(8,128)}, f32[2,6,6,16]{3,1,0,2:T(8,128)S(1)}, u32[]{:S(2)}, u32[]{:S(2)}) collective-permute-start(f32[2,6,6,16]{3,1,0,2:T(8,128)} %collective-permute-done.25), channel_id=1, source_target_pairs={{0,16},{4,20},{8,24},{12,28},{16,0},{20,4},{24,8},{28,12},{1,17},{... | collective-permute-start | bytes 13832 | tf_op jit(solution)/shard_map/ppermute | solution.py:26
  272.0 5.4 %collective-permute-start.23 = (f32[2,6,12,16]{3,1,0,2:T(8,128)S(1)}, f32[2,6,12,16]{3,1,0,2:T(8,128)S(1)}, u32[]{:S(2)}, u32[]{:S(2)}) collective-permute-start(f32[2,6,12,16]{3,1,0,2:T(8,128)S(1)} %collective-permute-done.22), channel_id=1, source_target_pairs={{0,2},{1,3},{2,0},{3,1},{4,6},{5,7},{6,4},{7,5},{8,10},{9,11},{10,... | collective-permute-start | bytes 27656 | tf_op jit(solution)/shard_map/ppermute | solution.py:26
  (24 other events, 624.4 us)
where the time goes:
time: 282 us
  blocking collectives  184 us (65%)
  starting transfers between devices  50.7 us (18%)
  local copies, waits for them, and re-layouts  15.3 us (5%)
  waiting for transfers between devices  13.8 us (5%)
  other arithmetic  9.88 us (4%)
  matrix products  5.9 us (2%)
    psum x3, blocking collectives, padded_tile(): summed_cols = lax.psum(cross_cols, 'tx')  116 us
    psum x3, blocking collectives, padded_tile(): row_block = lax.psum(col_sides, 'ty')  35 us
    psum x3, blocking collectives, padded_tile(): summed_rows = lax.psum(cross_rows, 'ty')  33.1 us
    ppermute x15, starting transfers between devices, partner(): return lax.ppermute(value, axis, pairs)  24.2 us
    ppermute x6, starting transfers between devices, extended(): before = lax.ppermute(last, axis, up)  18.7 us
    ppermute x15, waiting for transfers between devices, partner(): return lax.ppermute(value, axis, pairs)  11.6 us
    ppermute x6, starting transfers between devices, extended(): after = lax.ppermute(first, axis, down)  7.74 us
    gather x12, local copies, waits for them, and re-layouts, window_piece(): picked = jnp.take(held_block, jnp.clip(local_index, 0, length - 1), axis=2)  6.65 us
  transfers between devices with their start and end apart: 27, of which 10 were waited for; matrix products, arithmetic and copies ran while one was open for 5% of the time, Pallas kernels for 0%

commit v1 on v0

--- a/solution.py
+++ b/solution.py
@@ -115,7 +115,7 @@
             window_piece(row_block, side_cells - 1 - col_positions, row_index * tile_rows),
         ]
     )
-    summed_cols = lax.psum(cross_cols, "tx")
+    summed_cols = jnp.sum(lax.all_gather(cross_cols, "tx"), axis=0)
     cross_rows = jnp.stack(
         [
             window_piece(col_block, row_positions, col_index * tile_cols),

time: 282 us -> 353 us (1.25)
  blocking collectives: 184 us -> 245 us
  starting transfers between devices: 50.7 us -> 44.4 us
  other arithmetic: 9.88 us -> 16.1 us
  waiting for transfers between devices: 13.8 us -> 18 us
  local copies, waits for them, and re-layouts: 15.3 us -> 19.2 us
    all_gather x0 -> x3, blocking collectives: none -> 99.1 us  [padded_tile(): summed_cols = jnp.sum(lax.all_gather(cross_cols, 'tx'), axis=0)]
    psum x6 -> x3, blocking collectives: 149 us -> 111 us  [padded_tile(): col_block = lax.psum(row_sides, 'tx')]
    ppermute x6, starting transfers between devices: 18.7 us -> 10.5 us  [extended(): before = lax.ppermute(last, axis, up)]
    ppermute x6, waiting for transfers between devices: 0.02 us -> 7.81 us  [extended(): after = lax.ppermute(first, axis, down)]
  transfers between devices with their start and end apart: 27 -> 27, of which waited for: 10 -> 8; matrix products, arithmetic and copies ran while one was open for 5% -> 6% of each run, Pallas kernels for 0% -> 0%
where the time goes in v1:
time: 353 us; the launch traced here: 352 us
  blocking collectives  245 us (69%)
  starting transfers between devices  44.4 us (13%)
  local copies, waits for them, and re-layouts  19.2 us (5%)
  waiting for transfers between devices  18 us (5%)
  other arithmetic  16.1 us (5%)
  matrix products  7.39 us (2%)
    psum x3, blocking collectives, padded_tile(): col_block = lax.psum(row_sides, 'tx')  111 us
    all_gather x3, blocking collectives, padded_tile(): summed_cols = jnp.sum(lax.all_gather(cross_cols, 'tx'), axis=0)  99.1 us
    psum x3, blocking collectives, padded_tile(): row_block = lax.psum(col_sides, 'ty')  34.6 us
    ppermute x15, starting transfers between devices, partner(): return lax.ppermute(value, axis, pairs)  26.2 us
    ppermute x6, starting transfers between devices, extended(): before = lax.ppermute(last, axis, up)  10.5 us
    ppermute x15, waiting for transfers between devices, partner(): return lax.ppermute(value, axis, pairs)  10.1 us
    ppermute x6, waiting for transfers between devices, extended(): after = lax.ppermute(first, axis, down)  7.81 us
    ppermute x6, starting transfers between devices, extended(): after = lax.ppermute(first, axis, down)  7.75 us
  transfers between devices with their start and end apart: 27, of which 8 were waited for; matrix products, arithmetic and copies ran while one was open for 6% of the time, Pallas kernels for 0%

profile of v1, /device:TPU:0, one launch (start us, length us, event | category | flops | bytes accessed | tf_op | source)
XLA Modules:
  0.0 352.2 jit_solution(15026205470763318783)
XLA Ops:
  1.8 1.8 fusion.17
  4.4 39.8 %psum.63 = f32[2,6,12,16]{3,1,0,2:T(8,128)S(1)} all-reduce(f32[2,6,12,16]{3,1,0,2:T(8,128)S(1)} %copy.91), channel_id=1, replica_groups=mesh['tx'=8,'ty'=4] {'tx'}, use_global_device_ids=true, to_apply=%region_0.0 | all-reduce | flops 2304 | bytes 18432 | tf_op jit(solution)/shard_map/psum | solution.py:108
  45.8 11.7 %all-reduce.10 = (f32[2,6,6,16]{3,1,0,2:T(8,128)S(1)}, f32[2,2,6,6,16]{4,2,1,3,0:T(8,128)S(1)}) all-reduce(f32[2,6,6,16]{3,1,0,2:T(8,128)S(1)} %copy_multiply_fusion.3, f32[2,2,6,6,16]{4,2,1,3,0:T(8,128)S(1)} %pad_maximum_fusion.7), channel_id=1, replica_groups=mesh['tx'=8,'ty'=4] {'ty'}, use_global_device_ids=true, to_apply=%region_1.0 | all-reduce | flops 3456 | bytes 27648 | tf_op jit(solution)/shard_map/psum | solution.py:109
  59.1 3.6 %collective-permute-start = (f32[6,1,12,16]{3,0,2,1:T(8,128)}, f32[6,1,12,16]{3,0,2,1:T(8,128)S(1)}, u32[]{:S(2)}, u32[]{:S(2)}) collective-permute-start(f32[6,1,12,16]{3,0,2,1:T(8,128)} %get-tuple-element.195), channel_id=1, source_target_pairs={{0,4},{4,8},{8,12},{12,16},{16,20},{20,24},{24,28},{1,5},{5,9},{9,... | collective-permute-start | bytes 13832 | tf_op jit(solution)/shard_map/ppermute | solution.py:17
  69.1 34.1 %all-gather = f32[16,2,6,12,16]{4,1,3,2,0:T(2,128)S(1)} all-gather(f32[2,2,6,12,16]{4,1,3,2,0:T(2,128)S(1)} %copy.93), channel_id=2, replica_groups=mesh['tx'=8,'ty'=4] {'tx'}, dimensions={0}, use_global_device_ids=true | all-gather | bytes 165888 | tf_op jit(solution)/shard_map/all_gather | solution.py:118
  112.1 3.9 %collective-permute-done.7 = f32[2,6,6,16]{3,1,0,2:T(8,128)S(1)} collective-permute-done((f32[2,6,6,16]{3,1,0,2:T(8,128)}, f32[2,6,6,16]{3,1,0,2:T(8,128)S(1)}, u32[]{:S(2)}, u32[]{:S(2)}) %collective-permute-start.7) | collective-permute-done | bytes 4640 | tf_op jit(solution)/shard_map/ppermute | solution.py:26
  116.1 5.4 %collective-permute-start.5 = (f32[2,6,12,16]{3,1,0,2:T(8,128)}, f32[2,6,12,16]{3,1,0,2:T(8,128)S(1)}, u32[]{:S(2)}, u32[]{:S(2)}) collective-permute-start(f32[2,6,12,16]{3,1,0,2:T(8,128)} %collective-permute-done.4), channel_id=1, source_target_pairs={{0,2},{1,3},{2,0},{3,1},{4,6},{5,7},{6,4},{7,5},{8,10},{9,11},{10,... | collective-permute-start | bytes 27656 | tf_op jit(solution)/shard_map/ppermute | solution.py:26
  121.9 2.4 collective-permute-done.5
  127.7 35.0 %psum.66 = f32[2,6,6,16]{3,1,0,2:T(8,128)S(1)} all-reduce(f32[2,6,6,16]{3,1,0,2:T(8,128)S(1)} %copy.104), channel_id=1, replica_groups=mesh['tx'=8,'ty'=4] {'tx'}, use_global_device_ids=true, to_apply=%region_7.10 | all-reduce | flops 1152 | bytes 9216 | tf_op jit(solution)/shard_map/psum | solution.py:108
  164.0 11.2 %all-reduce.9 = (f32[2,6,3,16]{3,1,0,2:T(8,128)S(1)}, f32[2,2,6,3,16]{4,2,1,3,0:T(8,128)S(1)}) all-reduce(f32[2,6,3,16]{3,1,0,2:T(8,128)S(1)} %maximum_multiply_fusion.4, f32[2,2,6,3,16]{4,2,1,3,0:T(8,128)S(1)} %pad_maximum_fusion.11), channel_id=1, replica_groups=mesh['tx'=8,'ty'=4] {'ty'}, use_global_device_ids=true, to_apply=%region_8.11 | all-reduce | flops 1728 | bytes 13824 | tf_op jit(solution)/shard_map/psum | solution.py:109
  177.1 31.5 %all-gather.1 = f32[16,2,6,6,16]{4,1,3,2,0:T(2,128)S(1)} all-gather(f32[2,2,6,6,16]{4,1,3,2,0:T(2,128)S(1)} %copy.106), channel_id=3, replica_groups=mesh['tx'=8,'ty'=4] {'tx'}, dimensions={0}, use_global_device_ids=true | all-gather | bytes 82944 | tf_op jit(solution)/shard_map/all_gather | solution.py:118
  212.0 4.2 %collective-permute-done.10 = f32[6,1,6,16]{3,0,1,2:T(8,128)S(1)} collective-permute-done((f32[6,1,6,16]{3,0,1,2:T(8,128)S(1)}, f32[6,1,6,16]{3,0,1,2:T(8,128)S(1)}, u32[]{:S(2)}, u32[]{:S(2)}) %collective-permute-start.10) | collective-permute-done | bytes 2336 | tf_op jit(solution)/shard_map/ppermute | solution.py:18
  219.4 3.4 collective-permute-start.13
  222.8 3.5 collective-permute-start.17
  226.4 3.2 collective-permute-start.14
  230.0 1.7 collective-permute-done.14
  235.0 36.3 %psum.69 = f32[2,6,12,16]{3,1,2,0:T(8,128)S(1)} all-reduce(f32[2,6,12,16]{3,1,2,0:T(8,128)S(1)} %maximum_multiply_fusion.1), channel_id=1, replica_groups=mesh['tx'=8,'ty'=4] {'tx'}, use_global_device_ids=true, to_apply=%region_11.16 | all-reduce | flops 2304 | bytes 18432 | tf_op jit(solution)/shard_map/psum | solution.py:108
  273.0 11.7 %all-reduce.8 = (f32[2,6,6,16]{3,1,0,2:T(8,128)S(1)}, f32[2,2,6,6,16]{4,2,1,3,0:T(8,128)S(1)}) all-reduce(f32[2,6,6,16]{3,1,0,2:T(8,128)S(1)} %maximum_multiply_fusion.3, f32[2,2,6,6,16]{4,2,1,3,0:T(8,128)S(1)} %pad_maximum_fusion.9), channel_id=1, replica_groups=mesh['tx'=8,'ty'=4] {'ty'}, use_global_device_ids=true, to_apply=%region_12.17 | all-reduce | flops 3456 | bytes 27648 | tf_op jit(solution)/shard_map/psum | solution.py:109
  288.6 33.5 %all-gather.2 = f32[16,2,6,12,16]{4,1,3,2,0:T(2,128)S(1)} all-gather(f32[2,2,6,12,16]{4,1,3,2,0:T(2,128)S(1)} %copy.117), channel_id=4, replica_groups=mesh['tx'=8,'ty'=4] {'tx'}, dimensions={0}, use_global_device_ids=true | all-gather | bytes 165888 | tf_op jit(solution)/shard_map/all_gather | solution.py:118
  328.5 3.6 %collective-permute-done.19 = f32[6,1,12,16]{3,0,2,1:T(8,128)S(1)} collective-permute-done((f32[6,1,12,16]{3,0,2,1:T(8,128)}, f32[6,1,12,16]{3,0,2,1:T(8,128)S(1)}, u32[]{:S(2)}, u32[]{:S(2)}) %collective-permute-start.19) | collective-permute-done | bytes 4640 | tf_op jit(solution)/shard_map/ppermute | solution.py:18
  336.0 3.5 collective-permute-start.22
  339.5 3.5 collective-permute-start.26
  343.1 3.0 collective-permute-start.23
  346.8 1.9 collective-permute-done.23
  (294 shorter events, 56.6 us)
Async XLA Ops:
  58.1 53.5 %collective-permute-start.6 = (f32[2,6,6,16]{3,1,0,2:T(8,128)}, f32[2,6,6,16]{3,1,0,2:T(8,128)}, u32[]{:S(2)}, u32[]{:S(2)}) collective-permute-start(f32[2,6,6,16]{3,1,0,2:T(8,128)} %rev.19), channel_id=1, source_target_pairs={{0,4},{4,0},{8,12},{12,8},{16,20},{20,16},{24,28},{28,24},{1,5},{5... | collective-permute-start | bytes 13832 | tf_op jit(solution)/shard_map/ppermute | solution.py:26
  58.7 57.3 %collective-permute-start.4 = (f32[2,6,12,16]{3,1,0,2:T(8,128)}, f32[2,6,12,16]{3,1,0,2:T(8,128)}, u32[]{:S(2)}, u32[]{:S(2)}) collective-permute-start(f32[2,6,12,16]{3,1,0,2:T(8,128)} %rev.18), channel_id=1, source_target_pairs={{0,1},{1,0},{2,3},{3,2},{4,5},{5,4},{6,7},{7,6},{8,9},{9,8},{10,11... | collective-permute-start | bytes 27656 | tf_op jit(solution)/shard_map/ppermute | solution.py:26
  59.1 49.9 %collective-permute-start = (f32[6,1,12,16]{3,0,2,1:T(8,128)}, f32[6,1,12,16]{3,0,2,1:T(8,128)S(1)}, u32[]{:S(2)}, u32[]{:S(2)}) collective-permute-start(f32[6,1,12,16]{3,0,2,1:T(8,128)} %get-tuple-element.195), channel_id=1, source_target_pairs={{0,4},{4,8},{8,12},{12,16},{16,20},{20,24},{24,28},{1,5},{5,9},{9,... | collective-permute-start | bytes 13832 | tf_op jit(solution)/shard_map/ppermute | solution.py:17
  62.7 46.2 %collective-permute-start.1 = (f32[6,1,12,16]{3,0,1,2:T(8,128)S(1)}, f32[6,1,12,16]{3,0,1,2:T(8,128)S(1)}, u32[]{:S(2)}, u32[]{:S(2)}) collective-permute-start(f32[6,1,12,16]{3,0,1,2:T(8,128)S(1)} %get-tuple-element.194), channel_id=1, source_target_pairs={{4,0},{8,4},{12,8},{16,12},{20,16},{24,20},{28,24},{5,1},{9,5},{13... | collective-permute-start | bytes 13832 | tf_op jit(solution)/shard_map/ppermute | solution.py:18
  109.0 7.0 %collective-permute-start.2 = (f32[6,8,1,16]{3,0,1,2:T(8,128)S(1)}, f32[6,8,1,16]{3,0,1,2:T(8,128)S(1)}, u32[]{:S(2)}, u32[]{:S(2)}) collective-permute-start(f32[6,8,1,16]{3,0,1,2:T(8,128)S(1)} %get-tuple-element.180), channel_id=1, source_target_pairs={{0,1},{1,2},{2,3},{4,5},{5,6},{6,7},{8,9},{9,10},{10,11},{12,13},{... | collective-permute-start | bytes 9224 | tf_op jit(solution)/shard_map/ppermute | solution.py:17
  110.3 5.7 %collective-permute-start.3 = (f32[6,8,1,16]{3,0,1,2:T(8,128)S(1)}, f32[6,8,1,16]{3,0,1,2:T(8,128)S(1)}, u32[]{:S(2)}, u32[]{:S(2)}) collective-permute-start(f32[6,8,1,16]{3,0,1,2:T(8,128)S(1)} %get-tuple-element.181), channel_id=1, source_target_pairs={{1,0},{2,1},{3,2},{5,4},{6,5},{7,6},{9,8},{10,9},{11,10},{13,12},{... | collective-permute-start | bytes 9224 | tf_op jit(solution)/shard_map/ppermute | solution.py:18
  111.6 4.4 %collective-permute-start.7 = (f32[2,6,6,16]{3,1,0,2:T(8,128)}, f32[2,6,6,16]{3,1,0,2:T(8,128)S(1)}, u32[]{:S(2)}, u32[]{:S(2)}) collective-permute-start(f32[2,6,6,16]{3,1,0,2:T(8,128)} %collective-permute-done.6), channel_id=1, source_target_pairs={{0,8},{4,12},{8,0},{12,4},{16,24},{20,28},{24,16},{28,20},{1,9},{5... | collective-permute-start | bytes 13832 | tf_op jit(solution)/shard_map/ppermute | solution.py:26
  115.9 5.5 %collective-permute-start.8 = (f32[2,6,6,16]{3,1,0,2:T(8,128)S(1)}, f32[2,6,6,16]{3,1,0,2:T(8,128)S(1)}, u32[]{:S(2)}, u32[]{:S(2)}) collective-permute-start(f32[2,6,6,16]{3,1,0,2:T(8,128)S(1)} %collective-permute-done.7), channel_id=1, source_target_pairs={{0,16},{4,20},{8,24},{12,28},{16,0},{20,4},{24,8},{28,12},{1,17},{... | collective-permute-start | bytes 13832 | tf_op jit(solution)/shard_map/ppermute | solution.py:26
  116.1 8.2 %collective-permute-start.5 = (f32[2,6,12,16]{3,1,0,2:T(8,128)}, f32[2,6,12,16]{3,1,0,2:T(8,128)S(1)}, u32[]{:S(2)}, u32[]{:S(2)}) collective-permute-start(f32[2,6,12,16]{3,1,0,2:T(8,128)} %collective-permute-done.4), channel_id=1, source_target_pairs={{0,2},{1,3},{2,0},{3,1},{4,6},{5,7},{6,4},{7,5},{8,10},{9,11},{10,... | collective-permute-start | bytes 27656 | tf_op jit(solution)/shard_map/ppermute | solution.py:26
  175.7 43.2 %collective-permute-start.15 = (f32[2,6,3,16]{3,1,0,2:T(8,128)S(1)}, f32[2,6,3,16]{3,1,0,2:T(8,128)S(1)}, u32[]{:S(2)}, u32[]{:S(2)}) collective-permute-start(f32[2,6,3,16]{3,1,0,2:T(8,128)S(1)} %rev.21), channel_id=1, source_target_pairs={{0,4},{4,0},{8,12},{12,8},{16,20},{20,16},{24,28},{28,24},{1,5},{5... | collective-permute-start | bytes 6920 | tf_op jit(solution)/shard_map/ppermute | solution.py:26
  210.5 5.7 %collective-permute-start.10 = (f32[6,1,6,16]{3,0,1,2:T(8,128)S(1)}, f32[6,1,6,16]{3,0,1,2:T(8,128)S(1)}, u32[]{:S(2)}, u32[]{:S(2)}) collective-permute-start(f32[6,1,6,16]{3,0,1,2:T(8,128)S(1)} %get-tuple-element.214), channel_id=1, source_target_pairs={{4,0},{8,4},{12,8},{16,12},{20,16},{24,20},{28,24},{5,1},{9,5},{13... | collective-permute-start | bytes 6920 | tf_op jit(solution)/shard_map/ppermute | solution.py:18
  216.2 10.1 %collective-permute-start.11 = (f32[6,5,1,16]{3,0,1,2:T(8,128)S(1)}, f32[6,5,1,16]{3,0,1,2:T(8,128)S(1)}, u32[]{:S(2)}, u32[]{:S(2)}) collective-permute-start(f32[6,5,1,16]{3,0,1,2:T(8,128)S(1)} %get-tuple-element.202), channel_id=1, source_target_pairs={{0,1},{1,2},{2,3},{4,5},{5,6},{6,7},{8,9},{9,10},{10,11},{12,13},{... | collective-permute-start | bytes 5768 | tf_op jit(solution)/shard_map/ppermute | solution.py:17
  217.5 8.8 %collective-permute-start.12 = (f32[6,5,1,16]{3,0,1,2:T(8,128)S(1)}, f32[6,5,1,16]{3,0,1,2:T(8,128)S(1)}, u32[]{:S(2)}, u32[]{:S(2)}) collective-permute-start(f32[6,5,1,16]{3,0,1,2:T(8,128)S(1)} %get-tuple-element.203), channel_id=1, source_target_pairs={{1,0},{2,1},{3,2},{5,4},{6,5},{7,6},{9,8},{10,9},{11,10},{13,12},{... | collective-permute-start | bytes 5768 | tf_op jit(solution)/shard_map/ppermute | solution.py:18
  219.4 7.0 %collective-permute-start.13 = (f32[2,6,6,16]{3,1,0,2:T(8,128)S(1)}, f32[2,6,6,16]{3,1,0,2:T(8,128)S(1)}, u32[]{:S(2)}, u32[]{:S(2)}) collective-permute-start(f32[2,6,6,16]{3,1,0,2:T(8,128)S(1)} %rev.20), channel_id=1, source_target_pairs={{0,1},{1,0},{2,3},{3,2},{4,5},{5,4},{6,7},{7,6},{8,9},{9,8},{10,11... | collective-permute-start | bytes 13832 | tf_op jit(solution)/shard_map/ppermute | solution.py:26
  222.8 6.8 %collective-permute-start.17 = (f32[2,6,3,16]{3,1,0,2:T(8,128)S(1)}, f32[2,6,3,16]{3,1,0,2:T(8,128)S(1)}, u32[]{:S(2)}, u32[]{:S(2)}) collective-permute-start(f32[2,6,3,16]{3,1,0,2:T(8,128)S(1)} %collective-permute-done.16), channel_id=1, source_target_pairs={{0,16},{4,20},{8,24},{12,28},{16,0},{20,4},{24,8},{28,12},{1,17},{... | collective-permute-start | bytes 6920 | tf_op jit(solution)/shard_map/ppermute | solution.py:26
  226.4 5.3 %collective-permute-start.14 = (f32[2,6,6,16]{3,1,0,2:T(8,128)S(1)}, f32[2,6,6,16]{3,1,0,2:T(8,128)S(1)}, u32[]{:S(2)}, u32[]{:S(2)}) collective-permute-start(f32[2,6,6,16]{3,1,0,2:T(8,128)S(1)} %collective-permute-done.13), channel_id=1, source_target_pairs={{0,2},{1,3},{2,0},{3,1},{4,6},{5,7},{6,4},{7,5},{8,10},{9,11},{10,... | collective-permute-start | bytes 13832 | tf_op jit(solution)/shard_map/ppermute | solution.py:26
  288.3 46.4 %collective-permute-start.24 = (f32[2,6,6,16]{3,1,0,2:T(8,128)}, f32[2,6,6,16]{3,1,0,2:T(8,128)}, u32[]{:S(2)}, u32[]{:S(2)}) collective-permute-start(f32[2,6,6,16]{3,1,0,2:T(8,128)} %rev.23), channel_id=1, source_target_pairs={{0,4},{4,0},{8,12},{12,8},{16,20},{20,16},{24,28},{28,24},{1,5},{5... | collective-permute-start | bytes 13832 | tf_op jit(solution)/shard_map/ppermute | solution.py:26
  325.9 6.2 %collective-permute-start.19 = (f32[6,1,12,16]{3,0,2,1:T(8,128)}, f32[6,1,12,16]{3,0,2,1:T(8,128)S(1)}, u32[]{:S(2)}, u32[]{:S(2)}) collective-permute-start(f32[6,1,12,16]{3,0,2,1:T(8,128)} %get-tuple-element.186), channel_id=1, source_target_pairs={{4,0},{8,4},{12,8},{16,12},{20,16},{24,20},{28,24},{5,1},{9,5},{13... | collective-permute-start | bytes 13832 | tf_op jit(solution)/shard_map/ppermute | solution.py:18
  332.1 10.9 %collective-permute-start.20 = (f32[6,8,1,16]{3,0,1,2:T(8,128)S(1)}, f32[6,8,1,16]{3,0,1,2:T(8,128)S(1)}, u32[]{:S(2)}, u32[]{:S(2)}) collective-permute-start(f32[6,8,1,16]{3,0,1,2:T(8,128)S(1)} %get-tuple-element.178), channel_id=1, source_target_pairs={{0,1},{1,2},{2,3},{4,5},{5,6},{6,7},{8,9},{9,10},{10,11},{12,13},{... | collective-permute-start | bytes 9224 | tf_op jit(solution)/shard_map/ppermute | solution.py:17
  333.4 9.6 %collective-permute-start.21 = (f32[6,8,1,16]{3,0,1,2:T(8,128)S(1)}, f32[6,8,1,16]{3,0,1,2:T(8,128)S(1)}, u32[]{:S(2)}, u32[]{:S(2)}) collective-permute-start(f32[6,8,1,16]{3,0,1,2:T(8,128)S(1)} %get-tuple-element.179), channel_id=1, source_target_pairs={{1,0},{2,1},{3,2},{5,4},{6,5},{7,6},{9,8},{10,9},{11,10},{13,12},{... | collective-permute-start | bytes 9224 | tf_op jit(solution)/shard_map/ppermute | solution.py:18
  334.7 4.8 %collective-permute-start.25 = (f32[2,6,6,16]{3,1,0,2:T(8,128)}, f32[2,6,6,16]{3,1,0,2:T(8,128)S(1)}, u32[]{:S(2)}, u32[]{:S(2)}) collective-permute-start(f32[2,6,6,16]{3,1,0,2:T(8,128)} %collective-permute-done.24), channel_id=1, source_target_pairs={{0,8},{4,12},{8,0},{12,4},{16,24},{20,28},{24,16},{28,20},{1,9},{5... | collective-permute-start | bytes 13832 | tf_op jit(solution)/shard_map/ppermute | solution.py:26
  336.0 7.1 %collective-permute-start.22 = (f32[2,6,12,16]{3,1,2,0:T(8,128)S(1)}, f32[2,6,12,16]{3,1,2,0:T(8,128)S(1)}, u32[]{:S(2)}, u32[]{:S(2)}) collective-permute-start(f32[2,6,12,16]{3,1,2,0:T(8,128)S(1)} %rev.22), channel_id=1, source_target_pairs={{0,1},{1,0},{2,3},{3,2},{4,5},{5,4},{6,7},{7,6},{8,9},{9,8},{10,11... | collective-permute-start | bytes 27656 | tf_op jit(solution)/shard_map/ppermute | solution.py:26
  339.5 6.8 %collective-permute-start.26 = (f32[2,6,6,16]{3,1,0,2:T(8,128)S(1)}, f32[2,6,6,16]{3,1,0,2:T(8,128)S(1)}, u32[]{:S(2)}, u32[]{:S(2)}) collective-permute-start(f32[2,6,6,16]{3,1,0,2:T(8,128)S(1)} %collective-permute-done.25), channel_id=1, source_target_pairs={{0,16},{4,20},{8,24},{12,28},{16,0},{20,4},{24,8},{28,12},{1,17},{... | collective-permute-start | bytes 13832 | tf_op jit(solution)/shard_map/ppermute | solution.py:26
  343.1 5.6 %collective-permute-start.23 = (f32[2,6,12,16]{3,1,2,0:T(8,128)S(1)}, f32[2,6,12,16]{3,1,2,0:T(8,128)S(1)}, u32[]{:S(2)}, u32[]{:S(2)}) collective-permute-start(f32[2,6,12,16]{3,1,2,0:T(8,128)S(1)} %collective-permute-done.22), channel_id=1, source_target_pairs={{0,2},{1,3},{2,0},{3,1},{4,6},{5,7},{6,4},{7,5},{8,10},{9,11},{10,... | collective-permute-start | bytes 27656 | tf_op jit(solution)/shard_map/ppermute | solution.py:26
  (58 other events, 1614.7 us)
